TPU v7x, 128 devices: a whole 4x4x4 slice. The times are simulated.
128 devices in a mesh: blk: 16 (over x_lo, z, core), kv: 8 (over y, x_hi).
Axes of the slice: x: 4 (x_hi: 2, x_lo: 2; x = x_hi * 2 + x_lo), y: 4, z: 4, core: 2. Of those that a mesh axis runs over, the one named last changes fastest.
Arguments:
- hidden: bfloat16 [4096, 2880], P('blk', 'kv'), may hold values from -6 to 6
- gain_attn: float32 [2880], replicated, may hold values from 0.25 to 1.75
- w_q: bfloat16 [2880, 4096], P(None, 'kv'), may hold values from -0.109375 to 0.109375
- w_k: bfloat16 [2880, 512], P(None, 'kv'), may hold values from -0.109375 to 0.109375
- w_v: bfloat16 [2880, 512], P(None, 'kv'), may hold values from -0.109375 to 0.109375
- sinks: float32 [64], P('kv'), may hold values from 3 to 9
- w_o: bfloat16 [4096, 2880], P('kv'), may hold values from -0.75 to 0.75
- gain_moe: float32 [2880], replicated, may hold values from 0.25 to 1.75
- w_router: bfloat16 [2880, 32], replicated, may hold values from -5.1 to 5.1
- w_gate: bfloat16 [32, 2880, 2880], P('blk', None, 'kv'), may hold values from -0.4375 to 0.4375
- w_up: bfloat16 [32, 2880, 2880], P('blk', None, 'kv'), may hold values from -0.4375 to 0.4375
- w_down: bfloat16 [32, 2880, 2880], P('blk', 'kv'), may hold values from -0.013671875 to 0.013671875
- kv_pool: bfloat16 [256, 128, 1024], P('blk', None, 'kv'), may hold values from -160 to 160
- page_table: int32 [16, 16], P('blk'), may hold values from 0 to 255, as said below
- lengths: int32 [16], P('blk'), may hold values from 1 to 2048, as said below
- routes: int32 [4096, 4], P('blk'), may hold values from 0 to 31, all different within a row; in each aligned block of 256 rows (0 to 255, 256 to 511, ...) at most 48 rows name the same one
Outputs:
- mixed: bfloat16 [4096, 2880], P('blk', 'kv')
Inputs may be any that keep to these rules, and one draw needn't show every extreme that they name: `page_table`: row r lists distinct pool pages, except that requests with equal r // 4 share their first pages: the same page numbers, all lying within the cached tokens of every request of the group. A page outside such a shared run belongs to one request only. `lengths`: some request has exactly 2048 cached tokens. `routes`: among the rows of one request no expert is named more than 48 times, a bound that some block reaches.
All inputs are finite; a program needn't handle non-finite values.
Results may differ from a plain program's by a relative error of at most 0.015.
The roundings to bfloat16 on the way count: a program that leaves them out, or rounds other values in their place, can miss the bound.
Values may be sent and summed in bfloat16 or wider, within the bound.
A program may use at most 128 MiB of HBM per device.

v0:
```python
import jax
import jax.numpy as jnp
from jax import lax
from jax.sharding import PartitionSpec as P
from jax.experimental import pallas as pl
from jax.experimental.pallas import tpu as pltpu

HD = 64
EXP_DEV = 2


epsilon = 1e-05
rope_base = 150000.0
clamp_limit = 7.0
glu_alpha = 1.702


def rms_scale(values, gain_vec):
    mean_sq = jnp.mean(values * values, axis=-1, keepdims=True)
    return values * lax.rsqrt(mean_sq + epsilon) * gain_vec


def rotate(vectors, positions):
    half_dim = vectors.shape[-1] // 2
    inv_freq = rope_base ** (-jnp.arange(half_dim, dtype=jnp.float32) / half_dim)
    angles = positions.astype(jnp.float32)[:, None] * inv_freq[None, :]
    cosines = jnp.cos(angles)[:, None, :]
    sines = jnp.sin(angles)[:, None, :]
    front_half = vectors[..., :half_dim]
    back_half = vectors[..., half_dim:]
    return jnp.concatenate(
        [front_half * cosines - back_half * sines, back_half * cosines + front_half * sines],
        axis=-1,
    )


def swiglu(gate_in, up_in):
    gate_in = jnp.minimum(gate_in, clamp_limit)
    up_in = jnp.clip(up_in, -clamp_limit, clamp_limit)
    return (up_in + 1.0) * gate_in * jax.nn.sigmoid(glu_alpha * gate_in)


def head_kernel(len_ref, sink_ref, q_ref, k_ref, v_ref, o_ref):
    head = pl.program_id(0)
    length = len_ref[0]
    scores = lax.dot_general(
        q_ref[0], k_ref[...], (((1,), (1,)), ((), ())), preferred_element_type=jnp.float32
    ) * HD ** (-0.5)
    tok_rows, key_count = scores.shape
    ctx_len = key_count - tok_rows
    row_ids = lax.broadcasted_iota(jnp.int32, scores.shape, 0)
    col_ids = lax.broadcasted_iota(jnp.int32, scores.shape, 1)
    cached_seen = (col_ids < ctx_len) & (col_ids < length)
    new_seen = (col_ids >= ctx_len) & (col_ids - ctx_len <= row_ids)
    scores = jnp.where(cached_seen | new_seen, scores, -jnp.inf)
    sink = sink_ref[head]
    row_top = jnp.maximum(jnp.max(scores, axis=1, keepdims=True), sink)
    exp_terms = jnp.exp(scores - row_top)
    denom_sum = jnp.sum(exp_terms, axis=1, keepdims=True) + jnp.exp(sink - row_top)
    weights_attn = (exp_terms / denom_sum).astype(jnp.bfloat16)
    o_ref[0] = jnp.dot(weights_attn, v_ref[...], preferred_element_type=jnp.float32).astype(
        o_ref.dtype
    )


def attend(normed, length, page_rows, w_q, w_k, w_v, sinks):
    tok_rows = normed.shape[0]
    heads = w_q.shape[1] // HD
    positions = length + jnp.arange(tok_rows, dtype=jnp.int32)
    queries = jnp.dot(normed, w_q, preferred_element_type=jnp.float32).reshape(tok_rows, heads, HD)
    queries = rotate(queries, positions).astype(jnp.bfloat16).transpose(1, 0, 2)
    key_new = jnp.dot(normed, w_k, preferred_element_type=jnp.float32).reshape(tok_rows, 1, HD)
    key_new = rotate(key_new, positions).astype(jnp.bfloat16).reshape(tok_rows, HD)
    value_new = jnp.dot(normed, w_v, preferred_element_type=jnp.float32).astype(jnp.bfloat16)
    cached = page_rows.reshape(-1, 2, HD)
    key_all = jnp.concatenate([cached[:, 0], key_new], axis=0)
    value_all = jnp.concatenate([cached[:, 1], value_new], axis=0)
    keys = key_all.shape[0]
    attended = pl.pallas_call(
        head_kernel,
        out_shape=jax.ShapeDtypeStruct((heads, tok_rows, HD), jnp.bfloat16),
        grid_spec=pltpu.PrefetchScalarGridSpec(
            num_scalar_prefetch=2,
            grid=(heads,),
            in_specs=[
                pl.BlockSpec((1, tok_rows, HD), lambda h, n, s: (h, 0, 0)),
                pl.BlockSpec((keys, HD), lambda h, n, s: (0, 0)),
                pl.BlockSpec((keys, HD), lambda h, n, s: (0, 0)),
            ],
            out_specs=pl.BlockSpec((1, tok_rows, HD), lambda h, n, s: (h, 0, 0)),
        ),
        cost_estimate=pl.CostEstimate(
            flops=4 * heads * tok_rows * keys * HD,
            transcendentals=heads * tok_rows * keys,
            bytes_accessed=2 * (2 * heads * tok_rows * HD + 2 * keys * HD),
        ),
    )(length.reshape(1), sinks, queries, key_all, value_all)
    return attended.transpose(1, 0, 2).reshape(tok_rows, heads * HD)


def expert_slots(route_rows, expert_count):
    expert_ids = route_rows.reshape(-1)
    one_hot = (expert_ids[:, None] == jnp.arange(expert_count, dtype=jnp.int32)[None, :]).astype(
        jnp.int32
    )
    earlier = jnp.cumsum(one_hot, axis=0) - one_hot
    return (expert_ids, jnp.sum(earlier * one_hot, axis=1))


def gather_kv(block):
    count = lax.axis_size("kv")
    spread = jnp.broadcast_to(block[None], (count,) + block.shape)
    return lax.all_to_all(spread, "kv", 0, 0, tiled=True)


def reduce_kv(stacked):
    parts = lax.all_to_all(stacked, "kv", 0, 0, tiled=True)
    return jnp.sum(parts.astype(jnp.float32), axis=0)


def split_columns(block, count):
    rows, width = block.shape
    return block.reshape(rows, count, width // count).transpose(1, 0, 2)


def join_columns(stacked):
    count, rows, width = stacked.shape
    return stacked.transpose(1, 0, 2).reshape(rows, count * width)


def widen_rows(weight, count, pad):
    lead, depth, width = weight.shape
    weight = weight.reshape(lead, count, depth // count, width)
    weight = jnp.pad(weight, ((0, 0), (0, 0), (0, pad), (0, 0)))
    return weight.reshape(lead, count * (depth // count + pad), width)


def widen_cols(weight, count, pad):
    lead, depth, width = weight.shape
    weight = weight.reshape(lead, depth, count, width // count)
    weight = jnp.pad(weight, ((0, 0), (0, 0), (0, 0), (0, pad)))
    return weight.reshape(lead, depth, count * (width // count + pad))


def local(
    hidden,
    gain_attn,
    w_q,
    w_k,
    w_v,
    sinks,
    w_o,
    gain_moe,
    w_router,
    w_gate,
    w_up,
    w_down,
    kv_pool,
    page_table,
    lengths,
    routes,
):
    tok_rows = hidden.shape[0]
    slice_width = hidden.shape[1]
    kv_rank = lax.axis_index("kv")
    kv_count = lax.axis_size("kv")
    full_rows = join_columns(gather_kv(hidden))
    states = full_rows.astype(jnp.float32)
    normed = rms_scale(states, gain_attn).astype(jnp.bfloat16)
    pool_all = lax.all_gather(kv_pool, "blk", axis=0, tiled=True)
    page_rows = jnp.take(pool_all, page_table[0], axis=0)
    page_rows = page_rows.reshape(page_rows.shape[0] * page_rows.shape[1], -1)
    attended = attend(normed, lengths[0], page_rows, w_q, w_k, w_v, sinks)
    partial_value = jnp.dot(attended, w_o, preferred_element_type=jnp.float32)
    shared = reduce_kv(split_columns(partial_value.astype(jnp.bfloat16), kv_count))
    residual_slice = hidden.astype(jnp.float32) + shared
    total_sq = jnp.sum(gather_kv(jnp.sum(residual_slice * residual_slice, axis=1)), axis=0)
    gain_slice = lax.dynamic_slice_in_dim(gain_moe, kv_rank * slice_width, slice_width, 0)
    moe_slice_in = (
        residual_slice
        * lax.rsqrt(total_sq[:, None] / (slice_width * lax.axis_size("kv")) + epsilon)
        * gain_slice
    ).astype(jnp.bfloat16)
    top_count = routes.shape[1]
    blk_count = lax.axis_size("blk")
    blk_rank = lax.axis_index("blk")
    experts = EXP_DEV * blk_count
    capacity = max(2, 3 * tok_rows * top_count // (2 * experts))
    slots = experts * capacity
    pad = (-slice_width) % 128
    wide = slice_width + pad
    expert_ids, slot_ids = expert_slots(routes, experts)
    places = (expert_ids * capacity + slot_ids).reshape(tok_rows, top_count)
    slot_index = jnp.arange(slots, dtype=jnp.int32)
    picks = places[:, :, None] == slot_index[None, None, :]
    dispatch = jnp.any(picks, axis=1).astype(jnp.bfloat16)
    moe_wide = jnp.pad(moe_slice_in, ((0, 0), (0, pad)))
    outgoing = jnp.dot(dispatch.T, moe_wide, preferred_element_type=jnp.float32).astype(
        jnp.bfloat16
    )
    outgoing = outgoing.reshape(blk_count, EXP_DEV * capacity, wide)
    items = lax.all_to_all(outgoing, "blk", 0, 0, tiled=True)
    items = items.reshape(blk_count, EXP_DEV, capacity, wide).transpose(1, 0, 2, 3)
    items = items.reshape(EXP_DEV, blk_count * capacity, wide)
    gate_w = widen_rows(w_gate, kv_count, pad).reshape(EXP_DEV, kv_count, wide, -1)
    up_w = widen_rows(w_up, kv_count, pad).reshape(EXP_DEV, kv_count, wide, -1)
    down_w = widen_cols(w_down, kv_count, pad).reshape(EXP_DEV, -1, kv_count, wide)
    router_cols = lax.dynamic_slice_in_dim(w_router, blk_rank * EXP_DEV, EXP_DEV, 1)
    router_cols = widen_rows(router_cols.T[:, :, None], kv_count, pad)[:, :, 0]
    router_cols = router_cols.reshape(EXP_DEV, kv_count, wide)
    outs, chosen = [], []
    for el in range(EXP_DEV):
        with jax.named_scope(f"expert_{el}"):
            rows = gather_kv(items[el])
            gate_val = jnp.einsum("ird,idf->rf", rows, gate_w[el], preferred_element_type=jnp.float32)
            up_val = jnp.einsum("ird,idf->rf", rows, up_w[el], preferred_element_type=jnp.float32)
            act = swiglu(gate_val, up_val).astype(jnp.bfloat16)
            part = jnp.einsum(
                "rf,fid->ird", act, down_w[el], preferred_element_type=jnp.float32
            ).astype(jnp.bfloat16)
            outs.append(reduce_kv(part)[:, :slice_width].astype(jnp.bfloat16))
            chosen.append(
                jnp.einsum("ird,id->r", rows, router_cols[el], preferred_element_type=jnp.float32)
            )
    expert_out = jnp.concatenate(outs, axis=0)
    chosen = jnp.concatenate(chosen, axis=0).reshape(slots, 1)
    high = chosen.astype(jnp.bfloat16)
    rest = chosen - high.astype(jnp.float32)
    middle = rest.astype(jnp.bfloat16)
    low = (rest - middle.astype(jnp.float32)).astype(jnp.bfloat16)
    filler = jnp.zeros((slots, pad - 3), jnp.bfloat16)
    expert_out = jnp.concatenate([expert_out, high, middle, low, filler], axis=1)
    expert_out = expert_out.reshape(EXP_DEV, blk_count, capacity, wide).transpose(1, 0, 2, 3)
    expert_out = expert_out.reshape(blk_count, EXP_DEV * capacity, wide)
    arrived = lax.all_to_all(expert_out, "blk", 0, 0, tiled=True)
    arrived = arrived.reshape(slots, wide)
    picked = jnp.einsum(
        "tkp,pd->tkd", picks.astype(jnp.bfloat16), arrived, preferred_element_type=jnp.float32
    )
    logits = (
        picked[:, :, slice_width] + picked[:, :, slice_width + 1]
    ) + picked[:, :, slice_width + 2]
    weights = jax.nn.softmax(logits, axis=1)
    moe_slice = jnp.einsum("tk,tkd->td", weights, picked[:, :, :slice_width])
    return (residual_slice + moe_slice).astype(jnp.bfloat16)


def solution(mesh):
    in_specs = (
        P("blk", "kv"),
        P(),
        P(None, "kv"),
        P(None, "kv"),
        P(None, "kv"),
        P("kv"),
        P("kv", None),
        P(),
        P(),
        P("blk", None, "kv"),
        P("blk", None, "kv"),
        P("blk", "kv", None),
        P("blk", None, "kv"),
        P("blk", None),
        P("blk"),
        P("blk", None),
    )
    out_specs = P("blk", "kv")
    return jax.shard_map(local, mesh=mesh, in_specs=in_specs, out_specs=out_specs, check_vma=False)
```

profile of v0, /device:TPU:0, one launch (start us, length us, event | category | flops | bytes accessed | tf_op | source)
XLA Modules:
  0.0 453.4 jit_solution(11811107334791752838)
XLA Ops:
  9.6 7.0 %all-to-all-start = ((bf16[8,256,360]{1,2,0:T(8,128)(2,1)}), bf16[8,256,360]{1,2,0:T(8,128)(2,1)}, u32[]{:S(2)}, u32[]{:S(2)}) async-start(bf16[8,256,360]{1,2,0:T(8,128)(2,1)} %broadcast_in_dim.28), calls=%async_computation | async-start | bytes 2949120 | tf_op jit(solution)/shard_map/all_to_all | solution.py:113
  22.7 29.3 %all-to-all-done = bf16[8,256,360]{1,2,0:T(8,128)(2,1)} async-done(((bf16[8,256,360]{1,2,0:T(8,128)(2,1)}), bf16[8,256,360]{1,2,0:T(8,128)(2,1)}, u32[]{:S(2)}, u32[]{:S(2)}) %all-to-all-start) | async-done | bytes 1474592 | tf_op jit(solution)/shard_map/all_to_all | solution.py:113
  66.5 8.1 %all-gather.2.cloned.1.call-done = bf16[256,128,128]{2,1,0:T(8,128)(2,1)} async-done(((bf16[16,128,128]{2,1,0:T(8,128)(2,1)}), bf16[256,128,128]{2,1,0:T(8,128)(2,1)}) %all-gather.2.cloned.1.call-update) | async-done | bytes 8388624 | tf_op jit(solution)/shard_map/all_gather | solution.py:170
  83.0 14.1 %shard_map.154 = bf16[8,256,64]{2,1,0:T(8,128)(2,1)} custom-call(s32[1]{0:T(128)} %copy.212.len_ref, f32[8]{0:T(128)} %sink_ref.1, bf16[8,256,64]{2,1,0:T(8,128)(2,1)} %maximum_bitcast_fusion.q_ref, bf16[2304,64]{1,0:T(8,128)(2,1)} %get-tuple-element.21.k_ref, bf16[2304,64]{1,0:T(8,128)(2,1)} %get-tuple-element.22.v_ref), custom_call_target="tpu_custom_call" | custom-call | flops 1207959552 | bytes 1114112 | tf_op jit(solution)/shard_map/pallas_call | solution.py:79
  100.3 7.7 %all-to-all-start.1 = ((bf16[8,256,360]{1,2,0:T(8,128)(2,1)}), bf16[8,256,360]{1,2,0:T(8,128)(2,1)S(1)}, u32[]{:S(2)}, u32[]{:S(2)}) async-start(bf16[8,256,360]{1,2,0:T(8,128)(2,1)} %bitcast.239), calls=%async_computation.1 | async-start | bytes 2949120 | tf_op jit(solution)/shard_map/all_to_all | solution.py:117
  108.4 9.0 %reduce-window.6 = s32[32,8,128]{2,1,0:T(8,128)S(1)} reduce-window(s32[32,8,128]{2,1,0:T(8,128)S(1)} %fusion.101, s32[]{:T(128)} %constant.16.clone.1), window={size=1x1x128 pad=0_0x0_0x127_0}, to_apply=%region_2.3 | reduce-window | flops 4161536 | bytes 262148 | tf_op jit(solution)/shard_map/reduce-window
  118.2 12.1 %all-to-all-done.1 = bf16[8,256,360]{1,2,0:T(8,128)(2,1)S(1)} async-done(((bf16[8,256,360]{1,2,0:T(8,128)(2,1)}), bf16[8,256,360]{1,2,0:T(8,128)(2,1)S(1)}, u32[]{:S(2)}, u32[]{:S(2)}) %all-to-all-start.1) | async-done | bytes 1474592 | tf_op jit(solution)/shard_map/all_to_all | solution.py:117
  136.7 5.4 %all-to-all-done.2 = f32[8,1,256]{2,1,0:T(1,128)S(1)} async-done(((f32[8,1,256]{2,1,0:T(1,128)}), f32[8,1,256]{2,1,0:T(1,128)S(1)}, u32[]{:S(2)}, u32[]{:S(2)}) %all-to-all-start.2) | async-done | bytes 8224 | tf_op jit(solution)/shard_map/all_to_all | solution.py:113
  142.9 23.2 %all_to_all.46 = bf16[16,96,384]{2,1,0:T(8,128)(2,1)S(1)} all-to-all(bf16[16,96,384]{2,1,0:T(8,128)(2,1)S(1)} %bitcast.241), channel_id=1, replica_groups=mesh['blk'=16,'kv'=8] {'blk'}, dimensions={0} | all-to-all | bytes 2359296 | tf_op jit(solution)/shard_map/all_to_all | solution.py:202
  166.6 60.1 %all_to_all.47 = bf16[8,768,384]{2,1,0:T(8,128)(2,1)} all-to-all(bf16[8,768,384]{2,1,0:T(8,128)(2,1)S(1)} %broadcast_in_dim.35), channel_id=1, replica_groups=mesh['blk'=16,'kv'=8] {'kv'}, dimensions={0} | all-to-all | bytes 9437184 | tf_op jit(solution)/shard_map/expert_0/all_to_all | solution.py:113
  234.0 6.5 %copy.184 = bf16[2,2880,360]{2,1,0:T(8,128)(2,1)} copy(bf16[2,2880,360]{1,2,0:T(8,128)(2,1)} %param.25) | data formatting | bytes 8294400 | tf_op args[9]
  240.5 6.5 %copy.185 = bf16[2,8,360,360]{2,3,1,0:T(8,128)(2,1)} copy(bf16[2,8,360,360]{3,2,1,0:T(8,128)(2,1)} %bitcast.229) | data formatting | bytes 8294400 | tf_op jit(solution)/shard_map/reshape | solution.py:133
  247.0 6.5 %copy.182 = bf16[2,2880,360]{2,1,0:T(8,128)(2,1)} copy(bf16[2,2880,360]{1,2,0:T(8,128)(2,1)} %param.26) | data formatting | bytes 8294400 | tf_op args[10]
  253.4 6.5 %copy.183 = bf16[2,8,360,360]{2,3,1,0:T(8,128)(2,1)} copy(bf16[2,8,360,360]{3,2,1,0:T(8,128)(2,1)} %bitcast.230) | data formatting | bytes 8294400 | tf_op jit(solution)/shard_map/reshape | solution.py:133
  259.9 6.5 %copy.179 = bf16[2,360,2880]{1,2,0:T(8,128)(2,1)} copy(bf16[2,360,2880]{2,1,0:T(8,128)(2,1)} %param.27) | data formatting | bytes 8294400 | tf_op args[11]
  266.4 6.5 %copy.180 = bf16[2,360,8,360]{3,1,2,0:T(8,128)(2,1)} copy(bf16[2,360,8,360]{1,3,2,0:T(8,128)(2,1)} %bitcast.231) | data formatting | bytes 8294400 | tf_op jit(solution)/shard_map/reshape | solution.py:140
  272.9 5.0 %fusion.40 = f32[768,360]{0,1:T(8,128)S(1)} fusion(bf16[8,768,384]{2,1,0:T(8,128)(2,1)} %all_to_all.47, bf16[2,8,360,360]{2,3,1,0:T(8,128)(2,1)} %copy.185), kind=kOutput, calls=%fused_computation.39 | convolution fusion | flops 1698969600 | bytes 9971712 | tf_op jit(solution)/shard_map/expert_0/ird,idf->rf/dot_general | solution.py:215
  277.8 10.5 %convert_bitcast_fusion.1 = bf16[8,768,384]{1,2,0:T(8,128)(2,1)} fusion(bf16[2,360,8,360]{3,1,2,0:T(8,128)(2,1)} %copy.180, f32[768,360]{0,1:T(8,128)S(1)} %fusion.40, bf16[8,768,384]{2,1,0:T(8,128)(2,1)} %all_to_all.47, bf16[2,8,360,360]{2,3,1,0:T(8,128)(2,1)} %copy.183), kind=kOutput, calls=%fused_computation.5 | convolution fusion | flops 3402233856 | bytes 18837504 | tf_op jit(solution)/shard_map/expert_0/rf,fid->ird/dot_general | solution.py:218
  289.7 5.7 %all-to-all-start.5 = ((bf16[8,768,384]{1,2,0:T(8,128)(2,1)}), bf16[8,768,384]{1,2,0:T(8,128)(2,1)}, u32[]{:S(2)}, u32[]{:S(2)}) async-start(bf16[8,768,384]{1,2,0:T(8,128)(2,1)} %convert_bitcast_fusion.1), calls=%async_computation.5 | async-start | bytes 9437184 | tf_op jit(solution)/shard_map/expert_0/all_to_all | solution.py:117
  295.5 5.0 %fusion.43 = f32[768,360]{0,1:T(8,128)S(1)} fusion(bf16[8,768,384]{2,1,0:T(8,128)(2,1)} %all-to-all-done.6, bf16[2,8,360,360]{2,3,1,0:T(8,128)(2,1)} %copy.185), kind=kOutput, calls=%fused_computation.40 | convolution fusion | flops 1698969600 | bytes 9971712 | tf_op jit(solution)/shard_map/expert_1/ird,idf->rf/dot_general | solution.py:215
  300.4 10.5 %convert_bitcast_fusion = bf16[8,768,384]{1,2,0:T(8,128)(2,1)} fusion(bf16[2,360,8,360]{3,1,2,0:T(8,128)(2,1)} %copy.180, f32[768,360]{0,1:T(8,128)S(1)} %fusion.43, bf16[8,768,384]{2,1,0:T(8,128)(2,1)} %all-to-all-done.6, bf16[2,8,360,360]{2,3,1,0:T(8,128)(2,1)} %copy.183), kind=kOutput, calls=%fused_computation.4 | convolution fusion | flops 3402233856 | bytes 18837504 | tf_op jit(solution)/shard_map/expert_1/rf,fid->ird/dot_general | solution.py:218
  310.9 39.8 %all-to-all-done.5 = bf16[8,768,384]{1,2,0:T(8,128)(2,1)} async-done(((bf16[8,768,384]{1,2,0:T(8,128)(2,1)}), bf16[8,768,384]{1,2,0:T(8,128)(2,1)}, u32[]{:S(2)}, u32[]{:S(2)}) %all-to-all-start.5) | async-done | bytes 4718624 | tf_op jit(solution)/shard_map/expert_0/all_to_all | solution.py:117
  370.1 40.1 %all-to-all-done.7 = bf16[8,768,384]{1,2,0:T(8,128)(2,1)} async-done(((bf16[8,768,384]{1,2,0:T(8,128)(2,1)}), bf16[8,768,384]{1,2,0:T(8,128)(2,1)}, u32[]{:S(2)}, u32[]{:S(2)}) %all-to-all-start.7) | async-done | bytes 4718624 | tf_op jit(solution)/shard_map/expert_1/all_to_all | solution.py:117
  418.2 21.3 %all_to_all.48 = bf16[16,96,384]{2,1,0:T(8,128)(2,1)S(1)} all-to-all(bf16[16,96,384]{2,1,0:T(8,128)(2,1)S(1)} %bitcast.233), channel_id=1, replica_groups=mesh['blk'=16,'kv'=8] {'blk'}, dimensions={0} | all-to-all | bytes 2359296 | tf_op jit(solution)/shard_map/all_to_all | solution.py:235
  (114 shorter events, 86.2 us)
Async XLA Ops:
  6.5 91.7 %copy-start = (bf16[512,2880]{0,1:T(8,128)(2,1)S(1)}, bf16[512,2880]{0,1:T(8,128)(2,1)}, u32[]{:S(2)}) copy-start(bf16[512,2880]{0,1:T(8,128)(2,1)} %param.22) | copy-start | bytes 8847364
  6.5 68.0 %all-gather.2.cloned.1.call-start = ((), (), s32[]{:S(2)}) async-start(), calls=%async_computation.9 | async-start | bytes 8912896 | tf_op jit(solution)/shard_map/all_gather | solution.py:170
  7.3 10.0 %copy-start.10 = (f32[2880]{0:T(1024)S(1)}, f32[2880]{0:T(1024)}, u32[]{:S(2)}) copy-start(f32[2880]{0:T(1024)} %param.17) | copy-start | bytes 34564
  9.6 42.4 %all-to-all-start = ((bf16[8,256,360]{1,2,0:T(8,128)(2,1)}), bf16[8,256,360]{1,2,0:T(8,128)(2,1)}, u32[]{:S(2)}, u32[]{:S(2)}) async-start(bf16[8,256,360]{1,2,0:T(8,128)(2,1)} %broadcast_in_dim.28), calls=%async_computation | async-start | bytes 2949120 | tf_op jit(solution)/shard_map/all_to_all | solution.py:113
  17.4 4.7 %copy-start.12 = (s32[1,16]{1,0:T(1,128)S(1)}, s32[1,16]{1,0:T(1,128)}, u32[]{:S(2)}) copy-start(s32[1,16]{1,0:T(1,128)} %param.29) | copy-start | bytes 196
  52.0 4.9 %copy-start.6 = (bf16[2880,64]{0,1:T(8,128)(2,1)S(1)}, bf16[2880,64]{0,1:T(8,128)(2,1)}, u32[]{:S(2)}) copy-start(bf16[2880,64]{0,1:T(8,128)(2,1)} %param.20) | copy-start | bytes 1105924
  55.8 1.1 copy-start.2
  63.0 1.6 copy-start.3
  63.1 1.6 copy-start.7
  80.0 1.6 copy-start.8
  80.0 1.6 copy-start.9
  100.3 7.7 %copy-start.11 = (s32[256,4]{0,1:T(4,128)S(1)}, s32[256,4]{0,1:T(4,128)}, u32[]{:S(2)}) copy-start(s32[256,4]{0,1:T(4,128)} %param.31) | copy-start | bytes 12292
  100.3 29.9 %all-to-all-start.1 = ((bf16[8,256,360]{1,2,0:T(8,128)(2,1)}), bf16[8,256,360]{1,2,0:T(8,128)(2,1)S(1)}, u32[]{:S(2)}, u32[]{:S(2)}) async-start(bf16[8,256,360]{1,2,0:T(8,128)(2,1)} %bitcast.239), calls=%async_computation.1 | async-start | bytes 2949120 | tf_op jit(solution)/shard_map/all_to_all | solution.py:117
  108.0 22.4 %copy-start.4 = (bf16[256,360]{0,1:T(8,128)(2,1)S(1)}, bf16[256,360]{0,1:T(8,128)(2,1)}, u32[]{:S(2)}) copy-start(bf16[256,360]{0,1:T(8,128)(2,1)} %param.16) | copy-start | bytes 552964
  131.1 11.0 %all-to-all-start.2 = ((f32[8,1,256]{2,1,0:T(1,128)}), f32[8,1,256]{2,1,0:T(1,128)S(1)}, u32[]{:S(2)}, u32[]{:S(2)}) async-start(f32[8,1,256]{2,1,0:T(1,128)} %broadcast_in_dim.33), calls=%async_computation.2 | async-start | bytes 16384 | tf_op jit(solution)/shard_map/all_to_all | solution.py:113
  229.4 60.4 %all-to-all-start.6 = ((bf16[8,768,384]{2,1,0:T(8,128)(2,1)}), bf16[8,768,384]{2,1,0:T(8,128)(2,1)}, u32[]{:S(2)}, u32[]{:S(2)}) async-start(bf16[8,768,384]{2,1,0:T(8,128)(2,1)} %broadcast_in_dim.68), calls=%async_computation.6 | async-start | bytes 9437184 | tf_op jit(solution)/shard_map/expert_1/all_to_all | solution.py:113
  289.7 61.0 %all-to-all-start.5 = ((bf16[8,768,384]{1,2,0:T(8,128)(2,1)}), bf16[8,768,384]{1,2,0:T(8,128)(2,1)}, u32[]{:S(2)}, u32[]{:S(2)}) async-start(bf16[8,768,384]{1,2,0:T(8,128)(2,1)} %convert_bitcast_fusion.1), calls=%async_computation.5 | async-start | bytes 9437184 | tf_op jit(solution)/shard_map/expert_0/all_to_all | solution.py:117
  350.7 59.5 %all-to-all-start.7 = ((bf16[8,768,384]{1,2,0:T(8,128)(2,1)}), bf16[8,768,384]{1,2,0:T(8,128)(2,1)}, u32[]{:S(2)}, u32[]{:S(2)}) async-start(bf16[8,768,384]{1,2,0:T(8,128)(2,1)} %convert_bitcast_fusion), calls=%async_computation.7 | async-start | bytes 9437184 | tf_op jit(solution)/shard_map/expert_1/all_to_all | solution.py:117
  413.7 1.6 copy-start.5
  441.3 5.3 %copy-start.1 = (bf16[512,2880]{0,1:T(8,128)(2,1)S(1)}, bf16[512,2880]{0,1:T(8,128)(2,1)}, u32[]{:S(2)}) copy-start(bf16[512,2880]{0,1:T(8,128)(2,1)} %param.22) | copy-start | bytes 8847364
Sparse Core Ops, SparseCore 0:
  9.0 65.4 all-gather.1
where the time goes:
time: 456 us; the launch traced here: 453 us
  waiting for transfers between devices  137 us (30%)
  blocking collectives  105 us (23%)
  local copies, waits for them, and re-layouts  69.9 us (15%)
  matrix products  47.6 us (10%)
  starting transfers between devices  33.2 us (7%)
  other arithmetic  32.8 us (7%)
  between operations  14.5 us (3%)
  Pallas kernels  14.1 us (3%)
    all_to_all x3, waiting for transfers between devices, reduce_kv(): parts = lax.all_to_all(stacked, 'kv', 0, 0, tiled=True)  92 us
    all_to_all x1, blocking collectives, gather_kv(): return lax.all_to_all(spread, 'kv', 0, 0, tiled=True)  60.1 us
    all_to_all x3, waiting for transfers between devices, gather_kv(): return lax.all_to_all(spread, 'kv', 0, 0, tiled=True)  36.1 us
    unnamed x31, local copies, waits for them, and re-layouts  25.4 us
    all_to_all x1, blocking collectives, local(): items = lax.all_to_all(outgoing, 'blk', 0, 0, tiled=True)  23.2 us
    all_to_all x1, blocking collectives, local(): arrived = lax.all_to_all(expert_out, 'blk', 0, 0, tiled=True)  21.3 us
    dot_general x2, matrix products, local(): jnp.einsum('rf,fid->ird', act, down_w[el], preferred_element_type=jnp.flo...  21 us
    all_to_all x3, starting transfers between devices, reduce_kv(): parts = lax.all_to_all(stacked, 'kv', 0, 0, tiled=True)  18 us
  transfers between devices with their start and end apart: 7, of which 7 were waited for; matrix products, arithmetic and copies ran while one was open for 26% of the time, Pallas kernels for 0%

commit v1 on v0

--- a/solution.py
+++ b/solution.py
@@ -40,30 +40,55 @@
     return (up_in + 1.0) * gate_in * jax.nn.sigmoid(glu_alpha * gate_in)
 
 
-def head_kernel(len_ref, sink_ref, q_ref, k_ref, v_ref, o_ref):
+def head_kernel(len_ref, sink_ref, page_ref, q_ref, kn_ref, vn_ref, pool_ref, o_ref, pages, sems):
     head = pl.program_id(0)
+    page_rows = pool_ref.shape[1]
+    page_count = page_ref.shape[0]
+
+    @pl.when(head == 0)
+    def _():
+        copies = [
+            pltpu.make_async_copy(
+                pool_ref.at[page_ref[i]], pages.at[pl.ds(i * page_rows, page_rows)], sems.at[i]
+            )
+            for i in range(page_count)
+        ]
+        for copy in copies:
+            copy.start()
+        for copy in copies:
+            copy.wait()
+
     length = len_ref[0]
-    scores = lax.dot_general(
-        q_ref[0], k_ref[...], (((1,), (1,)), ((), ())), preferred_element_type=jnp.float32
-    ) * HD ** (-0.5)
-    tok_rows, key_count = scores.shape
-    ctx_len = key_count - tok_rows
-    row_ids = lax.broadcasted_iota(jnp.int32, scores.shape, 0)
-    col_ids = lax.broadcasted_iota(jnp.int32, scores.shape, 1)
-    cached_seen = (col_ids < ctx_len) & (col_ids < length)
-    new_seen = (col_ids >= ctx_len) & (col_ids - ctx_len <= row_ids)
-    scores = jnp.where(cached_seen | new_seen, scores, -jnp.inf)
+    query = q_ref[0]
+    ctx_keys = pages[:, :HD]
+    ctx_values = pages[:, HD:]
+    dims = (((1,), (1,)), ((), ()))
+    scale = HD ** (-0.5)
+    s_ctx = lax.dot_general(query, ctx_keys, dims, preferred_element_type=jnp.float32) * scale
+    s_new = lax.dot_general(query, kn_ref[...], dims, preferred_element_type=jnp.float32) * scale
+    ctx_cols = lax.broadcasted_iota(jnp.int32, s_ctx.shape, 1)
+    s_ctx = jnp.where(ctx_cols < length, s_ctx, -jnp.inf)
+    new_rows = lax.broadcasted_iota(jnp.int32, s_new.shape, 0)
+    new_cols = lax.broadcasted_iota(jnp.int32, s_new.shape, 1)
+    s_new = jnp.where(new_cols <= new_rows, s_new, -jnp.inf)
     sink = sink_ref[head]
-    row_top = jnp.maximum(jnp.max(scores, axis=1, keepdims=True), sink)
-    exp_terms = jnp.exp(scores - row_top)
-    denom_sum = jnp.sum(exp_terms, axis=1, keepdims=True) + jnp.exp(sink - row_top)
-    weights_attn = (exp_terms / denom_sum).astype(jnp.bfloat16)
-    o_ref[0] = jnp.dot(weights_attn, v_ref[...], preferred_element_type=jnp.float32).astype(
-        o_ref.dtype
-    )
-
-
-def attend(normed, length, page_rows, w_q, w_k, w_v, sinks):
+    row_top = jnp.maximum(
+        jnp.maximum(jnp.max(s_ctx, axis=1, keepdims=True), jnp.max(s_new, axis=1, keepdims=True)),
+        sink,
+    )
+    e_ctx = jnp.exp(s_ctx - row_top)
+    e_new = jnp.exp(s_new - row_top)
+    denom_sum = (
+        jnp.sum(e_ctx, axis=1, keepdims=True) + jnp.sum(e_new, axis=1, keepdims=True)
+    ) + jnp.exp(sink - row_top)
+    p_ctx = (e_ctx / denom_sum).astype(jnp.bfloat16)
+    p_new = (e_new / denom_sum).astype(jnp.bfloat16)
+    out = jnp.dot(p_ctx, ctx_values, preferred_element_type=jnp.float32)
+    out = out + jnp.dot(p_new, vn_ref[...], preferred_element_type=jnp.float32)
+    o_ref[0] = out.astype(o_ref.dtype)
+
+
+def attend(normed, length, page_ids, pool_all, w_q, w_k, w_v, sinks):
     tok_rows = normed.shape[0]
     heads = w_q.shape[1] // HD
     positions = length + jnp.arange(tok_rows, dtype=jnp.int32)
@@ -72,29 +97,34 @@
     key_new = jnp.dot(normed, w_k, preferred_element_type=jnp.float32).reshape(tok_rows, 1, HD)
     key_new = rotate(key_new, positions).astype(jnp.bfloat16).reshape(tok_rows, HD)
     value_new = jnp.dot(normed, w_v, preferred_element_type=jnp.float32).astype(jnp.bfloat16)
-    cached = page_rows.reshape(-1, 2, HD)
-    key_all = jnp.concatenate([cached[:, 0], key_new], axis=0)
-    value_all = jnp.concatenate([cached[:, 1], value_new], axis=0)
-    keys = key_all.shape[0]
+    page_count = page_ids.shape[0]
+    page_rows, page_width = pool_all.shape[1], pool_all.shape[2]
+    keys = page_count * page_rows + tok_rows
     attended = pl.pallas_call(
         head_kernel,
         out_shape=jax.ShapeDtypeStruct((heads, tok_rows, HD), jnp.bfloat16),
         grid_spec=pltpu.PrefetchScalarGridSpec(
-            num_scalar_prefetch=2,
+            num_scalar_prefetch=3,
             grid=(heads,),
             in_specs=[
-                pl.BlockSpec((1, tok_rows, HD), lambda h, n, s: (h, 0, 0)),
-                pl.BlockSpec((keys, HD), lambda h, n, s: (0, 0)),
-                pl.BlockSpec((keys, HD), lambda h, n, s: (0, 0)),
+                pl.BlockSpec((1, tok_rows, HD), lambda h, n, s, t: (h, 0, 0)),
+                pl.BlockSpec((tok_rows, HD), lambda h, n, s, t: (0, 0)),
+                pl.BlockSpec((tok_rows, HD), lambda h, n, s, t: (0, 0)),
+                pl.BlockSpec(memory_space=pl.ANY),
             ],
-            out_specs=pl.BlockSpec((1, tok_rows, HD), lambda h, n, s: (h, 0, 0)),
+            out_specs=pl.BlockSpec((1, tok_rows, HD), lambda h, n, s, t: (h, 0, 0)),
+            scratch_shapes=[
+                pltpu.VMEM((page_count * page_rows, page_width), jnp.bfloat16),
+                pltpu.SemaphoreType.DMA((page_count,)),
+            ],
         ),
+        compiler_params=pltpu.CompilerParams(dimension_semantics=("arbitrary",)),
         cost_estimate=pl.CostEstimate(
             flops=4 * heads * tok_rows * keys * HD,
             transcendentals=heads * tok_rows * keys,
             bytes_accessed=2 * (2 * heads * tok_rows * HD + 2 * keys * HD),
         ),
-    )(length.reshape(1), sinks, queries, key_all, value_all)
+    )(length.reshape(1), sinks, page_ids, queries, key_new, value_new, pool_all)
     return attended.transpose(1, 0, 2).reshape(tok_rows, heads * HD)
 
 
@@ -168,9 +198,7 @@
     states = full_rows.astype(jnp.float32)
     normed = rms_scale(states, gain_attn).astype(jnp.bfloat16)
     pool_all = lax.all_gather(kv_pool, "blk", axis=0, tiled=True)
-    page_rows = jnp.take(pool_all, page_table[0], axis=0)
-    page_rows = page_rows.reshape(page_rows.shape[0] * page_rows.shape[1], -1)
-    attended = attend(normed, lengths[0], page_rows, w_q, w_k, w_v, sinks)
+    attended = attend(normed, lengths[0], page_table[0], pool_all, w_q, w_k, w_v, sinks)
     partial_value = jnp.dot(attended, w_o, preferred_element_type=jnp.float32)
     shared = reduce_kv(split_columns(partial_value.astype(jnp.bfloat16), kv_count))
     residual_slice = hidden.astype(jnp.float32) + shared

time: 456 us -> 449 us (0.985)
  local copies, waits for them, and re-layouts: 69.9 us -> 64.9 us
    gather x2 -> x0, local copies, waits for them, and re-layouts: 5.43 us -> none  [local(): page_rows = jnp.take(pool_all, page_table[0], axis=0)]
    unnamed x31 -> x23, local copies, waits for them, and re-layouts: 25.4 us -> 25.3 us
where the time goes in v1:
time: 449 us; the launch traced here: 446 us
  waiting for transfers between devices  137 us (31%)
  blocking collectives  105 us (23%)
  local copies, waits for them, and re-layouts  64.9 us (14%)
  matrix products  47.1 us (10%)
  starting transfers between devices  33.2 us (7%)
  other arithmetic  30 us (7%)
  Pallas kernels  14.7 us (3%)
  between operations  14.5 us (3%)
    all_to_all x3, waiting for transfers between devices, reduce_kv(): parts = lax.all_to_all(stacked, 'kv', 0, 0, tiled=True)  92 us
    all_to_all x1, blocking collectives, gather_kv(): return lax.all_to_all(spread, 'kv', 0, 0, tiled=True)  60.1 us
    all_to_all x3, waiting for transfers between devices, gather_kv(): return lax.all_to_all(spread, 'kv', 0, 0, tiled=True)  36.2 us
    unnamed x23, local copies, waits for them, and re-layouts  25.3 us
    all_to_all x1, blocking collectives, local(): items = lax.all_to_all(outgoing, 'blk', 0, 0, tiled=True)  23.2 us
    all_to_all x1, blocking collectives, local(): arrived = lax.all_to_all(expert_out, 'blk', 0, 0, tiled=True)  21.2 us
    dot_general x2, matrix products, local(): jnp.einsum('rf,fid->ird', act, down_w[el], preferred_element_type=jnp.flo...  21 us
    all_to_all x3, starting transfers between devices, reduce_kv(): parts = lax.all_to_all(stacked, 'kv', 0, 0, tiled=True)  18 us
  transfers between devices with their start and end apart: 7, of which 7 were waited for; matrix products, arithmetic and copies ran while one was open for 26% of the time, Pallas kernels for 0%

profile of v1, /device:TPU:0, one launch (start us, length us, event | category | flops | bytes accessed | tf_op | source)
XLA Modules:
  0.0 445.7 jit_solution(3606462068470730259)
XLA Ops:
  9.6 7.0 %all-to-all-start = ((bf16[8,256,360]{1,2,0:T(8,128)(2,1)}), bf16[8,256,360]{1,2,0:T(8,128)(2,1)}, u32[]{:S(2)}, u32[]{:S(2)}) async-start(bf16[8,256,360]{1,2,0:T(8,128)(2,1)} %broadcast_in_dim.14), calls=%async_computation | async-start | bytes 2949120 | tf_op jit(solution)/shard_map/all_to_all | solution.py:143
  22.6 29.4 %all-to-all-done = bf16[8,256,360]{1,2,0:T(8,128)(2,1)} async-done(((bf16[8,256,360]{1,2,0:T(8,128)(2,1)}), bf16[8,256,360]{1,2,0:T(8,128)(2,1)}, u32[]{:S(2)}, u32[]{:S(2)}) %all-to-all-start) | async-done | bytes 1474592 | tf_op jit(solution)/shard_map/all_to_all | solution.py:143
  66.7 7.8 %all-gather.2.cloned.1.call-done.pool_ref = bf16[256,128,128]{2,1,0:T(8,128)(2,1)} async-done(((bf16[16,128,128]{2,1,0:T(8,128)(2,1)}), bf16[256,128,128]{2,1,0:T(8,128)(2,1)}) %all-gather.2.cloned.1.call-update) | async-done | bytes 8388624 | tf_op jit(solution)/shard_map/all_gather | solution.py:200
  74.5 14.7 %shard_map.154 = bf16[8,256,64]{2,1,0:T(8,128)(2,1)} custom-call(s32[1]{0:T(128)} %copy.195.len_ref, f32[8]{0:T(128)} %sink_ref.1, s32[16]{0:T(128)} %bitcast.236, bf16[8,256,64]{2,1,0:T(8,128)(2,1)} %maximum_bitcast_fusion.q_ref, bf16[256,64]{1,0:T(8,128)(2,1)} %pad_maximum_fusion.1.kn_ref, bf16[256,64]{1,0:T(8,128)(2,1)} %copy.158.vn_ref, ...), custom_call_target="tpu_custom_call" | custom-call | flops 1207959552 | bytes 1114112 | tf_op jit(solution)/shard_map/pallas_call | solution.py:103
  92.6 7.7 %all-to-all-start.1 = ((bf16[8,256,360]{1,2,0:T(8,128)(2,1)}), bf16[8,256,360]{1,2,0:T(8,128)(2,1)S(1)}, u32[]{:S(2)}, u32[]{:S(2)}) async-start(bf16[8,256,360]{1,2,0:T(8,128)(2,1)} %bitcast.229), calls=%async_computation.1 | async-start | bytes 2949120 | tf_op jit(solution)/shard_map/all_to_all | solution.py:147
  100.7 9.0 %reduce-window.6 = s32[32,8,128]{2,1,0:T(8,128)S(1)} reduce-window(s32[32,8,128]{2,1,0:T(8,128)S(1)} %fusion.101, s32[]{:T(128)} %constant.13.clone.1), window={size=1x1x128 pad=0_0x0_0x127_0}, to_apply=%region_2.0 | reduce-window | flops 4161536 | bytes 262148 | tf_op jit(solution)/shard_map/reduce-window
  110.4 12.0 %all-to-all-done.1 = bf16[8,256,360]{1,2,0:T(8,128)(2,1)S(1)} async-done(((bf16[8,256,360]{1,2,0:T(8,128)(2,1)}), bf16[8,256,360]{1,2,0:T(8,128)(2,1)S(1)}, u32[]{:S(2)}, u32[]{:S(2)}) %all-to-all-start.1) | async-done | bytes 1474592 | tf_op jit(solution)/shard_map/all_to_all | solution.py:147
  128.9 5.4 %all-to-all-done.2 = f32[8,1,256]{2,1,0:T(1,128)S(1)} async-done(((f32[8,1,256]{2,1,0:T(1,128)}), f32[8,1,256]{2,1,0:T(1,128)S(1)}, u32[]{:S(2)}, u32[]{:S(2)}) %all-to-all-start.2) | async-done | bytes 8224 | tf_op jit(solution)/shard_map/all_to_all | solution.py:143
  135.1 23.2 %all_to_all.46 = bf16[16,96,384]{2,1,0:T(8,128)(2,1)S(1)} all-to-all(bf16[16,96,384]{2,1,0:T(8,128)(2,1)S(1)} %bitcast.231), channel_id=1, replica_groups=mesh['blk'=16,'kv'=8] {'blk'}, dimensions={0} | all-to-all | bytes 2359296 | tf_op jit(solution)/shard_map/all_to_all | solution.py:230
  158.9 60.1 %all_to_all.47 = bf16[8,768,384]{2,1,0:T(8,128)(2,1)} all-to-all(bf16[8,768,384]{2,1,0:T(8,128)(2,1)S(1)} %broadcast_in_dim.17), channel_id=1, replica_groups=mesh['blk'=16,'kv'=8] {'kv'}, dimensions={0} | all-to-all | bytes 9437184 | tf_op jit(solution)/shard_map/expert_0/all_to_all | solution.py:143
  226.2 6.5 %copy.170 = bf16[2,2880,360]{2,1,0:T(8,128)(2,1)} copy(bf16[2,2880,360]{1,2,0:T(8,128)(2,1)} %param.25) | data formatting | bytes 8294400 | tf_op args[9]
  232.7 6.5 %copy.171 = bf16[2,8,360,360]{2,3,1,0:T(8,128)(2,1)} copy(bf16[2,8,360,360]{3,2,1,0:T(8,128)(2,1)} %bitcast.218) | data formatting | bytes 8294400 | tf_op jit(solution)/shard_map/reshape | solution.py:163
  239.2 6.5 %copy.168 = bf16[2,2880,360]{2,1,0:T(8,128)(2,1)} copy(bf16[2,2880,360]{1,2,0:T(8,128)(2,1)} %param.26) | data formatting | bytes 8294400 | tf_op args[10]
  245.7 6.5 %copy.169 = bf16[2,8,360,360]{2,3,1,0:T(8,128)(2,1)} copy(bf16[2,8,360,360]{3,2,1,0:T(8,128)(2,1)} %bitcast.219) | data formatting | bytes 8294400 | tf_op jit(solution)/shard_map/reshape | solution.py:163
  252.2 6.5 %copy.165 = bf16[2,360,2880]{1,2,0:T(8,128)(2,1)} copy(bf16[2,360,2880]{2,1,0:T(8,128)(2,1)} %param.27) | data formatting | bytes 8294400 | tf_op args[11]
  258.6 6.5 %copy.166 = bf16[2,360,8,360]{3,1,2,0:T(8,128)(2,1)} copy(bf16[2,360,8,360]{1,3,2,0:T(8,128)(2,1)} %bitcast.220) | data formatting | bytes 8294400 | tf_op jit(solution)/shard_map/reshape | solution.py:170
  265.1 5.0 %fusion.40 = f32[768,360]{0,1:T(8,128)S(1)} fusion(bf16[8,768,384]{2,1,0:T(8,128)(2,1)} %all_to_all.47, bf16[2,8,360,360]{2,3,1,0:T(8,128)(2,1)} %copy.171), kind=kOutput, calls=%fused_computation.38 | convolution fusion | flops 1698969600 | bytes 9971712 | tf_op jit(solution)/shard_map/expert_0/ird,idf->rf/dot_general | solution.py:243
  270.1 10.5 %convert_bitcast_fusion.1 = bf16[8,768,384]{1,2,0:T(8,128)(2,1)} fusion(bf16[2,360,8,360]{3,1,2,0:T(8,128)(2,1)} %copy.166, f32[768,360]{0,1:T(8,128)S(1)} %fusion.40, bf16[8,768,384]{2,1,0:T(8,128)(2,1)} %all_to_all.47, bf16[2,8,360,360]{2,3,1,0:T(8,128)(2,1)} %copy.169), kind=kOutput, calls=%fused_computation.4 | convolution fusion | flops 3402233856 | bytes 18837504 | tf_op jit(solution)/shard_map/expert_0/rf,fid->ird/dot_general | solution.py:246
  282.0 5.7 %all-to-all-start.5 = ((bf16[8,768,384]{1,2,0:T(8,128)(2,1)}), bf16[8,768,384]{1,2,0:T(8,128)(2,1)}, u32[]{:S(2)}, u32[]{:S(2)}) async-start(bf16[8,768,384]{1,2,0:T(8,128)(2,1)} %convert_bitcast_fusion.1), calls=%async_computation.5 | async-start | bytes 9437184 | tf_op jit(solution)/shard_map/expert_0/all_to_all | solution.py:147
  287.7 5.0 %fusion.43 = f32[768,360]{0,1:T(8,128)S(1)} fusion(bf16[8,768,384]{2,1,0:T(8,128)(2,1)} %all-to-all-done.6, bf16[2,8,360,360]{2,3,1,0:T(8,128)(2,1)} %copy.171), kind=kOutput, calls=%fused_computation.39 | convolution fusion | flops 1698969600 | bytes 9971712 | tf_op jit(solution)/shard_map/expert_1/ird,idf->rf/dot_general | solution.py:243
  292.7 10.5 %convert_bitcast_fusion = bf16[8,768,384]{1,2,0:T(8,128)(2,1)} fusion(bf16[2,360,8,360]{3,1,2,0:T(8,128)(2,1)} %copy.166, f32[768,360]{0,1:T(8,128)S(1)} %fusion.43, bf16[8,768,384]{2,1,0:T(8,128)(2,1)} %all-to-all-done.6, bf16[2,8,360,360]{2,3,1,0:T(8,128)(2,1)} %copy.169), kind=kOutput, calls=%fused_computation.3 | convolution fusion | flops 3402233856 | bytes 18837504 | tf_op jit(solution)/shard_map/expert_1/rf,fid->ird/dot_general | solution.py:246
  303.2 39.8 %all-to-all-done.5 = bf16[8,768,384]{1,2,0:T(8,128)(2,1)} async-done(((bf16[8,768,384]{1,2,0:T(8,128)(2,1)}), bf16[8,768,384]{1,2,0:T(8,128)(2,1)}, u32[]{:S(2)}, u32[]{:S(2)}) %all-to-all-start.5) | async-done | bytes 4718624 | tf_op jit(solution)/shard_map/expert_0/all_to_all | solution.py:147
  362.4 40.1 %all-to-all-done.7 = bf16[8,768,384]{1,2,0:T(8,128)(2,1)} async-done(((bf16[8,768,384]{1,2,0:T(8,128)(2,1)}), bf16[8,768,384]{1,2,0:T(8,128)(2,1)}, u32[]{:S(2)}, u32[]{:S(2)}) %all-to-all-start.7) | async-done | bytes 4718624 | tf_op jit(solution)/shard_map/expert_1/all_to_all | solution.py:147
  410.4 21.2 %all_to_all.48 = bf16[16,96,384]{2,1,0:T(8,128)(2,1)S(1)} all-to-all(bf16[16,96,384]{2,1,0:T(8,128)(2,1)S(1)} %bitcast.222), channel_id=1, replica_groups=mesh['blk'=16,'kv'=8] {'blk'}, dimensions={0} | all-to-all | bytes 2359296 | tf_op jit(solution)/shard_map/all_to_all | solution.py:263
  (98 shorter events, 78.0 us)
Async XLA Ops:
  6.5 84.0 %copy-start = (bf16[512,2880]{0,1:T(8,128)(2,1)S(1)}, bf16[512,2880]{0,1:T(8,128)(2,1)}, u32[]{:S(2)}) copy-start(bf16[512,2880]{0,1:T(8,128)(2,1)} %param.22) | copy-start | bytes 8847364
  6.5 68.0 %all-gather.2.cloned.1.call-start = ((), (), s32[]{:S(2)}) async-start(), calls=%async_computation.9 | async-start | bytes 8912896 | tf_op jit(solution)/shard_map/all_gather | solution.py:200
  7.3 10.0 %copy-start.7 = (f32[2880]{0:T(1024)S(1)}, f32[2880]{0:T(1024)}, u32[]{:S(2)}) copy-start(f32[2880]{0:T(1024)} %param.17) | copy-start | bytes 34564
  9.6 42.4 %all-to-all-start = ((bf16[8,256,360]{1,2,0:T(8,128)(2,1)}), bf16[8,256,360]{1,2,0:T(8,128)(2,1)}, u32[]{:S(2)}, u32[]{:S(2)}) async-start(bf16[8,256,360]{1,2,0:T(8,128)(2,1)} %broadcast_in_dim.14), calls=%async_computation | async-start | bytes 2949120 | tf_op jit(solution)/shard_map/all_to_all | solution.py:143
  52.0 4.9 %copy-start.6 = (bf16[2880,64]{0,1:T(8,128)(2,1)S(1)}, bf16[2880,64]{0,1:T(8,128)(2,1)}, u32[]{:S(2)}) copy-start(bf16[2880,64]{0,1:T(8,128)(2,1)} %param.20) | copy-start | bytes 1105924
  55.8 1.1 copy-start.2
  60.1 3.2 copy-start.3
  92.6 7.7 %copy-start.8 = (s32[256,4]{0,1:T(4,128)S(1)}, s32[256,4]{0,1:T(4,128)}, u32[]{:S(2)}) copy-start(s32[256,4]{0,1:T(4,128)} %param.31) | copy-start | bytes 12292
  92.6 29.9 %all-to-all-start.1 = ((bf16[8,256,360]{1,2,0:T(8,128)(2,1)}), bf16[8,256,360]{1,2,0:T(8,128)(2,1)S(1)}, u32[]{:S(2)}, u32[]{:S(2)}) async-start(bf16[8,256,360]{1,2,0:T(8,128)(2,1)} %bitcast.229), calls=%async_computation.1 | async-start | bytes 2949120 | tf_op jit(solution)/shard_map/all_to_all | solution.py:147
  100.2 22.4 %copy-start.4 = (bf16[256,360]{0,1:T(8,128)(2,1)S(1)}, bf16[256,360]{0,1:T(8,128)(2,1)}, u32[]{:S(2)}) copy-start(bf16[256,360]{0,1:T(8,128)(2,1)} %param.16) | copy-start | bytes 552964
  123.4 11.0 %all-to-all-start.2 = ((f32[8,1,256]{2,1,0:T(1,128)}), f32[8,1,256]{2,1,0:T(1,128)S(1)}, u32[]{:S(2)}, u32[]{:S(2)}) async-start(f32[8,1,256]{2,1,0:T(1,128)} %broadcast_in_dim.15), calls=%async_computation.2 | async-start | bytes 16384 | tf_op jit(solution)/shard_map/all_to_all | solution.py:143
  221.6 60.4 %all-to-all-start.6 = ((bf16[8,768,384]{2,1,0:T(8,128)(2,1)}), bf16[8,768,384]{2,1,0:T(8,128)(2,1)}, u32[]{:S(2)}, u32[]{:S(2)}) async-start(bf16[8,768,384]{2,1,0:T(8,128)(2,1)} %broadcast_in_dim.19), calls=%async_computation.6 | async-start | bytes 9437184 | tf_op jit(solution)/shard_map/expert_1/all_to_all | solution.py:143
  282.0 61.0 %all-to-all-start.5 = ((bf16[8,768,384]{1,2,0:T(8,128)(2,1)}), bf16[8,768,384]{1,2,0:T(8,128)(2,1)}, u32[]{:S(2)}, u32[]{:S(2)}) async-start(bf16[8,768,384]{1,2,0:T(8,128)(2,1)} %convert_bitcast_fusion.1), calls=%async_computation.5 | async-start | bytes 9437184 | tf_op jit(solution)/shard_map/expert_0/all_to_all | solution.py:147
  343.0 59.5 %all-to-all-start.7 = ((bf16[8,768,384]{1,2,0:T(8,128)(2,1)}), bf16[8,768,384]{1,2,0:T(8,128)(2,1)}, u32[]{:S(2)}, u32[]{:S(2)}) async-start(bf16[8,768,384]{1,2,0:T(8,128)(2,1)} %convert_bitcast_fusion), calls=%async_computation.7 | async-start | bytes 9437184 | tf_op jit(solution)/shard_map/expert_1/all_to_all | solution.py:147
  406.0 1.6 copy-start.5
  433.5 5.3 %copy-start.1 = (bf16[512,2880]{0,1:T(8,128)(2,1)S(1)}, bf16[512,2880]{0,1:T(8,128)(2,1)}, u32[]{:S(2)}) copy-start(bf16[512,2880]{0,1:T(8,128)(2,1)} %param.22) | copy-start | bytes 8847364
Sparse Core Ops, SparseCore 0:
  9.0 65.4 all-gather.1

commit v2 on v1

--- a/solution.py
+++ b/solution.py
@@ -40,7 +40,9 @@
     return (up_in + 1.0) * gate_in * jax.nn.sigmoid(glu_alpha * gate_in)
 
 
-def head_kernel(len_ref, sink_ref, page_ref, q_ref, kn_ref, vn_ref, pool_ref, o_ref, pages, sems):
+def head_kernel(
+    len_ref, sink_ref, page_ref, q_ref, kn_ref, vn_ref, pool_ref, wo_ref, o_ref, pages, sems, total
+):
     head = pl.program_id(0)
     page_rows = pool_ref.shape[1]
     page_count = page_ref.shape[0]
@@ -85,10 +87,23 @@
     p_new = (e_new / denom_sum).astype(jnp.bfloat16)
     out = jnp.dot(p_ctx, ctx_values, preferred_element_type=jnp.float32)
     out = out + jnp.dot(p_new, vn_ref[...], preferred_element_type=jnp.float32)
-    o_ref[0] = out.astype(o_ref.dtype)
-
-
-def attend(normed, length, page_ids, pool_all, w_q, w_k, w_v, sinks):
+    rows = wo_ref[pl.ds(pl.multiple_of(head * HD, HD), HD), :]
+    step = jnp.dot(out.astype(jnp.bfloat16), rows, preferred_element_type=jnp.float32)
+
+    @pl.when(head == 0)
+    def _():
+        total[...] = step
+
+    @pl.when(head > 0)
+    def _():
+        total[...] += step
+
+    @pl.when(head == pl.num_programs(0) - 1)
+    def _():
+        o_ref[...] = total[...].astype(o_ref.dtype)
+
+
+def attend(normed, length, page_ids, pool_all, w_q, w_k, w_v, sinks, w_o):
     tok_rows = normed.shape[0]
     heads = w_q.shape[1] // HD
     positions = length + jnp.arange(tok_rows, dtype=jnp.int32)
@@ -102,7 +117,7 @@
     keys = page_count * page_rows + tok_rows
     attended = pl.pallas_call(
         head_kernel,
-        out_shape=jax.ShapeDtypeStruct((heads, tok_rows, HD), jnp.bfloat16),
+        out_shape=jax.ShapeDtypeStruct((tok_rows, w_o.shape[1]), jnp.bfloat16),
         grid_spec=pltpu.PrefetchScalarGridSpec(
             num_scalar_prefetch=3,
             grid=(heads,),
@@ -111,11 +126,13 @@
                 pl.BlockSpec((tok_rows, HD), lambda h, n, s, t: (0, 0)),
                 pl.BlockSpec((tok_rows, HD), lambda h, n, s, t: (0, 0)),
                 pl.BlockSpec(memory_space=pl.ANY),
+                pl.BlockSpec(w_o.shape, lambda h, n, s, t: (0, 0)),
             ],
-            out_specs=pl.BlockSpec((1, tok_rows, HD), lambda h, n, s, t: (h, 0, 0)),
+            out_specs=pl.BlockSpec((tok_rows, w_o.shape[1]), lambda h, n, s, t: (0, 0)),
             scratch_shapes=[
                 pltpu.VMEM((page_count * page_rows, page_width), jnp.bfloat16),
                 pltpu.SemaphoreType.DMA((page_count,)),
+                pltpu.VMEM((tok_rows, w_o.shape[1]), jnp.float32),
             ],
         ),
         compiler_params=pltpu.CompilerParams(dimension_semantics=("arbitrary",)),
@@ -124,8 +141,8 @@
             transcendentals=heads * tok_rows * keys,
             bytes_accessed=2 * (2 * heads * tok_rows * HD + 2 * keys * HD),
         ),
-    )(length.reshape(1), sinks, page_ids, queries, key_new, value_new, pool_all)
-    return attended.transpose(1, 0, 2).reshape(tok_rows, heads * HD)
+    )(length.reshape(1), sinks, page_ids, queries, key_new, value_new, pool_all, w_o)
+    return attended
 
 
 def expert_slots(route_rows, expert_count):
@@ -198,9 +215,8 @@
     states = full_rows.astype(jnp.float32)
     normed = rms_scale(states, gain_attn).astype(jnp.bfloat16)
     pool_all = lax.all_gather(kv_pool, "blk", axis=0, tiled=True)
-    attended = attend(normed, lengths[0], page_table[0], pool_all, w_q, w_k, w_v, sinks)
-    partial_value = jnp.dot(attended, w_o, preferred_element_type=jnp.float32)
-    shared = reduce_kv(split_columns(partial_value.astype(jnp.bfloat16), kv_count))
+    partial_value = attend(normed, lengths[0], page_table[0], pool_all, w_q, w_k, w_v, sinks, w_o)
+    shared = reduce_kv(split_columns(partial_value, kv_count))
     residual_slice = hidden.astype(jnp.float32) + shared
     total_sq = jnp.sum(gather_kv(jnp.sum(residual_slice * residual_slice, axis=1)), axis=0)
     gain_slice = lax.dynamic_slice_in_dim(gain_moe, kv_rank * slice_width, slice_width, 0)

time: 449 us -> 453 us (level)
  Pallas kernels: 14.7 us -> 23.1 us
  other arithmetic: 30 us -> 24.6 us
    pallas_call x1, Pallas kernels: 14.7 us -> 23.1 us  [attend(): pl.pallas_call(head_kernel, out_shape=jax.ShapeDtypeStruct((tok_rows, w_o...]
    all_gather x1, waiting for transfers between devices: 7.85 us -> 13.8 us  [local(): pool_all = lax.all_gather(kv_pool, 'blk', axis=0, tiled=True)]
    all_to_all x3, waiting for transfers between devices: 36.2 us -> 30.8 us  [gather_kv(): return lax.all_to_all(spread, 'kv', 0, 0, tiled=True)]
    unnamed x23 -> x22, local copies, waits for them, and re-layouts: 25.3 us -> 28.9 us
where the time goes in v2:
time: 453 us; the launch traced here: 450 us
  waiting for transfers between devices  137 us (30%)
  blocking collectives  105 us (23%)
  local copies, waits for them, and re-layouts  68 us (15%)
  matrix products  44.6 us (10%)
  starting transfers between devices  33.2 us (7%)
  other arithmetic  24.6 us (5%)
  Pallas kernels  23.1 us (5%)
  between operations  14.5 us (3%)
    all_to_all x3, waiting for transfers between devices, reduce_kv(): parts = lax.all_to_all(stacked, 'kv', 0, 0, tiled=True)  92 us
    all_to_all x1, blocking collectives, gather_kv(): return lax.all_to_all(spread, 'kv', 0, 0, tiled=True)  60.1 us
    all_to_all x3, waiting for transfers between devices, gather_kv(): return lax.all_to_all(spread, 'kv', 0, 0, tiled=True)  30.8 us
    unnamed x22, local copies, waits for them, and re-layouts  28.9 us
    all_to_all x1, blocking collectives, local(): items = lax.all_to_all(outgoing, 'blk', 0, 0, tiled=True)  23.2 us
    pallas_call x1, Pallas kernels, attend(): pl.pallas_call(head_kernel, out_shape=jax.ShapeDtypeStruct((tok_rows, w_o...  23.1 us
    all_to_all x1, blocking collectives, local(): arrived = lax.all_to_all(expert_out, 'blk', 0, 0, tiled=True)  21.2 us
    dot_general x2, matrix products, local(): jnp.einsum('rf,fid->ird', act, down_w[el], preferred_element_type=jnp.flo...  21 us
  transfers between devices with their start and end apart: 7, of which 7 were waited for; matrix products, arithmetic and copies ran while one was open for 26% of the time, Pallas kernels for 0%

profile of v2, /device:TPU:0, one launch (start us, length us, event | category | flops | bytes accessed | tf_op | source)
XLA Modules:
  0.0 449.8 jit_solution(1140169869311129045)
XLA Ops:
  9.4 7.0 %all-to-all-start = ((bf16[8,256,360]{1,2,0:T(8,128)(2,1)}), bf16[8,256,360]{1,2,0:T(8,128)(2,1)S(1)}, u32[]{:S(2)}, u32[]{:S(2)}) async-start(bf16[8,256,360]{1,2,0:T(8,128)(2,1)} %broadcast_in_dim.14), calls=%async_computation | async-start | bytes 2949120 | tf_op jit(solution)/shard_map/all_to_all | solution.py:160
  27.6 23.9 %all-to-all-done = bf16[8,256,360]{1,2,0:T(8,128)(2,1)S(1)} async-done(((bf16[8,256,360]{1,2,0:T(8,128)(2,1)}), bf16[8,256,360]{1,2,0:T(8,128)(2,1)S(1)}, u32[]{:S(2)}, u32[]{:S(2)}) %all-to-all-start) | async-done | bytes 1474592 | tf_op jit(solution)/shard_map/all_to_all | solution.py:160
  60.5 13.8 %all-gather.2.cloned.1.call-done.pool_ref = bf16[256,128,128]{2,1,0:T(8,128)(2,1)} async-done(((bf16[16,128,128]{2,1,0:T(8,128)(2,1)}), bf16[256,128,128]{2,1,0:T(8,128)(2,1)}) %all-gather.2.cloned.1.call-update) | async-done | bytes 8388624 | tf_op jit(solution)/shard_map/all_gather | solution.py:217
  74.4 23.1 %shard_map.154 = bf16[256,2880]{1,0:T(8,128)(2,1)} custom-call(s32[1]{0:T(128)} %copy.203.len_ref, f32[8]{0:T(128)} %sink_ref.1, s32[16]{0:T(128)} %bitcast.229, bf16[8,256,64]{2,1,0:T(8,128)(2,1)} %maximum_bitcast_fusion.q_ref, bf16[256,64]{1,0:T(8,128)(2,1)} %pad_maximum_fusion.1.kn_ref, bf16[256,64]{1,0:T(8,128)(2,1)} %copy.165.vn_ref, ...), custom_call_target="tpu_custom_call" | custom-call | flops 1207959552 | bytes 1114112 | tf_op jit(solution)/shard_map/pallas_call | solution.py:118
  100.0 7.7 %all-to-all-start.1 = ((bf16[8,256,360]{1,2,0:T(8,128)(2,1)}), bf16[8,256,360]{1,2,0:T(8,128)(2,1)S(1)}, u32[]{:S(2)}, u32[]{:S(2)}) async-start(bf16[8,256,360]{1,2,0:T(8,128)(2,1)} %bitcast.14), calls=%async_computation.1 | async-start | bytes 2949120 | tf_op jit(solution)/shard_map/all_to_all | solution.py:164
  108.1 9.0 %reduce-window.6 = s32[32,8,128]{2,1,0:T(8,128)S(1)} reduce-window(s32[32,8,128]{2,1,0:T(8,128)S(1)} %fusion.101, s32[]{:T(128)} %constant.13.clone.1), window={size=1x1x128 pad=0_0x0_0x127_0}, to_apply=%region_2.0 | reduce-window | flops 4161536 | bytes 262148 | tf_op jit(solution)/shard_map/reduce-window
  117.9 12.0 %all-to-all-done.1 = bf16[8,256,360]{1,2,0:T(8,128)(2,1)S(1)} async-done(((bf16[8,256,360]{1,2,0:T(8,128)(2,1)}), bf16[8,256,360]{1,2,0:T(8,128)(2,1)S(1)}, u32[]{:S(2)}, u32[]{:S(2)}) %all-to-all-start.1) | async-done | bytes 1474592 | tf_op jit(solution)/shard_map/all_to_all | solution.py:164
  136.3 5.4 %all-to-all-done.2 = f32[8,1,256]{2,1,0:T(1,128)S(1)} async-done(((f32[8,1,256]{2,1,0:T(1,128)}), f32[8,1,256]{2,1,0:T(1,128)S(1)}, u32[]{:S(2)}, u32[]{:S(2)}) %all-to-all-start.2) | async-done | bytes 8224 | tf_op jit(solution)/shard_map/all_to_all | solution.py:160
  142.6 23.2 %all_to_all.46 = bf16[16,96,384]{2,1,0:T(8,128)(2,1)S(1)} all-to-all(bf16[16,96,384]{2,1,0:T(8,128)(2,1)S(1)} %bitcast.225), channel_id=1, replica_groups=mesh['blk'=16,'kv'=8] {'blk'}, dimensions={0} | all-to-all | bytes 2359296 | tf_op jit(solution)/shard_map/all_to_all | solution.py:246
  166.3 60.1 %all_to_all.47 = bf16[8,768,384]{2,1,0:T(8,128)(2,1)} all-to-all(bf16[8,768,384]{2,1,0:T(8,128)(2,1)S(1)} %broadcast_in_dim.17), channel_id=1, replica_groups=mesh['blk'=16,'kv'=8] {'kv'}, dimensions={0} | all-to-all | bytes 9437184 | tf_op jit(solution)/shard_map/expert_0/all_to_all | solution.py:160
  233.7 6.5 %copy.178 = bf16[2,2880,360]{2,1,0:T(8,128)(2,1)} copy(bf16[2,2880,360]{1,2,0:T(8,128)(2,1)} %param.25) | data formatting | bytes 8294400 | tf_op args[9]
  240.2 6.5 %copy.179 = bf16[2,8,360,360]{2,3,1,0:T(8,128)(2,1)} copy(bf16[2,8,360,360]{3,2,1,0:T(8,128)(2,1)} %bitcast.214) | data formatting | bytes 8294400 | tf_op jit(solution)/shard_map/reshape | solution.py:180
  246.7 6.5 %copy.176 = bf16[2,2880,360]{2,1,0:T(8,128)(2,1)} copy(bf16[2,2880,360]{1,2,0:T(8,128)(2,1)} %param.26) | data formatting | bytes 8294400 | tf_op args[10]
  253.1 6.5 %copy.177 = bf16[2,8,360,360]{2,3,1,0:T(8,128)(2,1)} copy(bf16[2,8,360,360]{3,2,1,0:T(8,128)(2,1)} %bitcast.215) | data formatting | bytes 8294400 | tf_op jit(solution)/shard_map/reshape | solution.py:180
  259.6 6.5 %copy.173 = bf16[2,360,2880]{1,2,0:T(8,128)(2,1)} copy(bf16[2,360,2880]{2,1,0:T(8,128)(2,1)} %param.27) | data formatting | bytes 8294400 | tf_op args[11]
  266.1 6.5 %copy.174 = bf16[2,360,8,360]{3,1,2,0:T(8,128)(2,1)} copy(bf16[2,360,8,360]{1,3,2,0:T(8,128)(2,1)} %bitcast.216) | data formatting | bytes 8294400 | tf_op jit(solution)/shard_map/reshape | solution.py:187
  272.6 5.0 %fusion.40 = f32[768,360]{0,1:T(8,128)S(1)} fusion(bf16[8,768,384]{2,1,0:T(8,128)(2,1)} %all_to_all.47, bf16[2,8,360,360]{2,3,1,0:T(8,128)(2,1)} %copy.179), kind=kOutput, calls=%fused_computation.37 | convolution fusion | flops 1698969600 | bytes 9971712 | tf_op jit(solution)/shard_map/expert_0/ird,idf->rf/dot_general | solution.py:259
  277.5 10.5 %convert_bitcast_fusion.1 = bf16[8,768,384]{1,2,0:T(8,128)(2,1)} fusion(bf16[2,360,8,360]{3,1,2,0:T(8,128)(2,1)} %copy.174, f32[768,360]{0,1:T(8,128)S(1)} %fusion.40, bf16[8,768,384]{2,1,0:T(8,128)(2,1)} %all_to_all.47, bf16[2,8,360,360]{2,3,1,0:T(8,128)(2,1)} %copy.177), kind=kOutput, calls=%fused_computation.4 | convolution fusion | flops 3402233856 | bytes 18837504 | tf_op jit(solution)/shard_map/expert_0/rf,fid->ird/dot_general | solution.py:262
  289.4 5.7 %all-to-all-start.5 = ((bf16[8,768,384]{1,2,0:T(8,128)(2,1)}), bf16[8,768,384]{1,2,0:T(8,128)(2,1)}, u32[]{:S(2)}, u32[]{:S(2)}) async-start(bf16[8,768,384]{1,2,0:T(8,128)(2,1)} %convert_bitcast_fusion.1), calls=%async_computation.5 | async-start | bytes 9437184 | tf_op jit(solution)/shard_map/expert_0/all_to_all | solution.py:164
  295.2 5.0 %fusion.43 = f32[768,360]{0,1:T(8,128)S(1)} fusion(bf16[8,768,384]{2,1,0:T(8,128)(2,1)} %all-to-all-done.6, bf16[2,8,360,360]{2,3,1,0:T(8,128)(2,1)} %copy.179), kind=kOutput, calls=%fused_computation.38 | convolution fusion | flops 1698969600 | bytes 9971712 | tf_op jit(solution)/shard_map/expert_1/ird,idf->rf/dot_general | solution.py:259
  300.1 10.5 %convert_bitcast_fusion = bf16[8,768,384]{1,2,0:T(8,128)(2,1)} fusion(bf16[2,360,8,360]{3,1,2,0:T(8,128)(2,1)} %copy.174, f32[768,360]{0,1:T(8,128)S(1)} %fusion.43, bf16[8,768,384]{2,1,0:T(8,128)(2,1)} %all-to-all-done.6, bf16[2,8,360,360]{2,3,1,0:T(8,128)(2,1)} %copy.177), kind=kOutput, calls=%fused_computation.3 | convolution fusion | flops 3402233856 | bytes 18837504 | tf_op jit(solution)/shard_map/expert_1/rf,fid->ird/dot_general | solution.py:262
  310.6 39.8 %all-to-all-done.5 = bf16[8,768,384]{1,2,0:T(8,128)(2,1)} async-done(((bf16[8,768,384]{1,2,0:T(8,128)(2,1)}), bf16[8,768,384]{1,2,0:T(8,128)(2,1)}, u32[]{:S(2)}, u32[]{:S(2)}) %all-to-all-start.5) | async-done | bytes 4718624 | tf_op jit(solution)/shard_map/expert_0/all_to_all | solution.py:164
  369.8 40.1 %all-to-all-done.7 = bf16[8,768,384]{1,2,0:T(8,128)(2,1)} async-done(((bf16[8,768,384]{1,2,0:T(8,128)(2,1)}), bf16[8,768,384]{1,2,0:T(8,128)(2,1)}, u32[]{:S(2)}, u32[]{:S(2)}) %all-to-all-start.7) | async-done | bytes 4718624 | tf_op jit(solution)/shard_map/expert_1/all_to_all | solution.py:164
  417.9 21.2 %all_to_all.48 = bf16[16,96,384]{2,1,0:T(8,128)(2,1)S(1)} all-to-all(bf16[16,96,384]{2,1,0:T(8,128)(2,1)S(1)} %bitcast.218), channel_id=1, replica_groups=mesh['blk'=16,'kv'=8] {'blk'}, dimensions={0} | all-to-all | bytes 2359296 | tf_op jit(solution)/shard_map/all_to_all | solution.py:279
  (96 shorter events, 73.2 us)
Async XLA Ops:
  6.5 45.9 %copy-start = (bf16[2880,64]{0,1:T(8,128)(2,1)S(1)}, bf16[2880,64]{0,1:T(8,128)(2,1)}, u32[]{:S(2)}) copy-start(bf16[2880,64]{0,1:T(8,128)(2,1)} %param.20) | copy-start | bytes 1105924
  6.5 67.8 %all-gather.2.cloned.1.call-start = ((), (), s32[]{:S(2)}) async-start(), calls=%async_computation.9 | async-start | bytes 8912896 | tf_op jit(solution)/shard_map/all_gather | solution.py:217
  7.3 9.8 %copy-start.6 = (f32[2880]{0:T(1024)S(1)}, f32[2880]{0:T(1024)}, u32[]{:S(2)}) copy-start(f32[2880]{0:T(1024)} %param.17) | copy-start | bytes 34564
  9.4 42.1 %all-to-all-start = ((bf16[8,256,360]{1,2,0:T(8,128)(2,1)}), bf16[8,256,360]{1,2,0:T(8,128)(2,1)S(1)}, u32[]{:S(2)}, u32[]{:S(2)}) async-start(bf16[8,256,360]{1,2,0:T(8,128)(2,1)} %broadcast_in_dim.14), calls=%async_computation | async-start | bytes 2949120 | tf_op jit(solution)/shard_map/all_to_all | solution.py:160
  55.2 1.9 copy-start.2
  57.1 1.8 copy-start.5
  100.0 7.7 %copy-start.7 = (s32[256,4]{0,1:T(4,128)S(1)}, s32[256,4]{0,1:T(4,128)}, u32[]{:S(2)}) copy-start(s32[256,4]{0,1:T(4,128)} %param.31) | copy-start | bytes 12292
  100.0 29.9 %all-to-all-start.1 = ((bf16[8,256,360]{1,2,0:T(8,128)(2,1)}), bf16[8,256,360]{1,2,0:T(8,128)(2,1)S(1)}, u32[]{:S(2)}, u32[]{:S(2)}) async-start(bf16[8,256,360]{1,2,0:T(8,128)(2,1)} %bitcast.14), calls=%async_computation.1 | async-start | bytes 2949120 | tf_op jit(solution)/shard_map/all_to_all | solution.py:164
  107.7 22.4 %copy-start.3 = (bf16[256,360]{0,1:T(8,128)(2,1)S(1)}, bf16[256,360]{0,1:T(8,128)(2,1)}, u32[]{:S(2)}) copy-start(bf16[256,360]{0,1:T(8,128)(2,1)} %param.16) | copy-start | bytes 552964
  130.8 11.0 %all-to-all-start.2 = ((f32[8,1,256]{2,1,0:T(1,128)}), f32[8,1,256]{2,1,0:T(1,128)S(1)}, u32[]{:S(2)}, u32[]{:S(2)}) async-start(f32[8,1,256]{2,1,0:T(1,128)} %broadcast_in_dim.15), calls=%async_computation.2 | async-start | bytes 16384 | tf_op jit(solution)/shard_map/all_to_all | solution.py:160
  229.1 60.4 %all-to-all-start.6 = ((bf16[8,768,384]{2,1,0:T(8,128)(2,1)}), bf16[8,768,384]{2,1,0:T(8,128)(2,1)}, u32[]{:S(2)}, u32[]{:S(2)}) async-start(bf16[8,768,384]{2,1,0:T(8,128)(2,1)} %broadcast_in_dim.19), calls=%async_computation.6 | async-start | bytes 9437184 | tf_op jit(solution)/shard_map/expert_1/all_to_all | solution.py:160
  289.4 61.0 %all-to-all-start.5 = ((bf16[8,768,384]{1,2,0:T(8,128)(2,1)}), bf16[8,768,384]{1,2,0:T(8,128)(2,1)}, u32[]{:S(2)}, u32[]{:S(2)}) async-start(bf16[8,768,384]{1,2,0:T(8,128)(2,1)} %convert_bitcast_fusion.1), calls=%async_computation.5 | async-start | bytes 9437184 | tf_op jit(solution)/shard_map/expert_0/all_to_all | solution.py:164
  350.4 59.5 %all-to-all-start.7 = ((bf16[8,768,384]{1,2,0:T(8,128)(2,1)}), bf16[8,768,384]{1,2,0:T(8,128)(2,1)}, u32[]{:S(2)}, u32[]{:S(2)}) async-start(bf16[8,768,384]{1,2,0:T(8,128)(2,1)} %convert_bitcast_fusion), calls=%async_computation.7 | async-start | bytes 9437184 | tf_op jit(solution)/shard_map/expert_1/all_to_all | solution.py:164
  441.0 1.1 copy-start.4
  441.0 1.9 copy-start.1
Sparse Core Ops, SparseCore 0:
  9.0 65.2 all-gather.1
